TPU v7x, 32 devices: a whole 2x2x4 slice. The times are simulated.
32 devices in a mesh: tm: 8 (over y, x, core), space: 4 (over z).
Axes of the slice: x: 2, y: 2, z: 4, core: 2. Of those that a mesh axis runs over, the one named last changes fastest.
Arguments:
- adjoint_iterate: float32 [64, 16, 32, 128], P('tm', None, 'space'), may hold values from -6 to 6
- innovations: float32 [64, 16, 512], P('tm', None, 'space'), may hold values from -6 to 6
- station_cells: int32 [64, 512], P('tm', 'space'), may hold values from 0 to 1023
- diffusivity: float32 [16, 32, 128], P(None, 'space'), may hold values from 0.01 to 0.08
- wind_x: float32 [16, 32, 128], P(None, 'space'), may hold values from -0.2 to 0.2
- wind_y: float32 [16, 32, 128], P(None, 'space'), may hold values from -0.2 to 0.2
- vertical_mixing: float32 [16, 32, 128], P(None, 'space'), may hold values from 0.01 to 0.1
Outputs:
- updated_iterate: float32 [64, 16, 32, 128], P('tm', None, 'space')
Inputs may be any that keep to these rules, and one draw needn't show every extreme that they name: `station_cells`: A station's column within its tile of 8 x 128 columns is numbered x * 128 + y; several stations may share a column.
All inputs are finite; a program needn't handle non-finite values.
Results may differ from a plain program's by a relative error of at most 0.0003.
Values sent between devices are 32-bit elements; how exact they have to be, the bound alone decides.
No kernel may reach another device: no remote copies, remote signals or barrier semaphores. Data moves between devices by JAX's collectives and lax.ppermute only.
A program may use at most 64 MiB of HBM per device.

v0:
```python
import math
import jax
import jax.numpy as jnp
from jax import lax
from jax.sharding import PartitionSpec as P

LEV = 16
TX = 8
NY = 128
STEPS_DEV = 8
INNER = 4
circ_alpha = 0.1


def from_behind(value, axis, steps):
    count = lax.axis_size(axis)
    leading, last = (max(0, -steps), min(count, count - steps))
    return lax.ppermute(value, axis, [(source, source + steps) for source in range(leading, last)])


def with_halo(cells, sides, width):
    for axis, dim in sides:
        count = lax.axis_size(axis)
        ends = count - 1
        head = lax.slice_in_dim(cells, 0, width, axis=dim)
        tail = lax.slice_in_dim(cells, cells.shape[dim] - width, cells.shape[dim], axis=dim)
        cells = jnp.concatenate(
            [
                lax.ppermute(tail, axis, [(i, (i + 1) % count) for i in range(ends)]),
                cells,
                lax.ppermute(head, axis, [((i + 1) % count, i) for i in range(ends)]),
            ],
            axis=dim,
        )
    return cells


def transfer_rates(diffusivity, wind_x, wind_y, vertical_mixing):
    east_rate = diffusivity + jnp.maximum(-wind_x, 0.0)
    west_rate = diffusivity + jnp.maximum(wind_x, 0.0)
    north_rate = diffusivity + jnp.maximum(-wind_y, 0.0)
    south_rate = diffusivity + jnp.maximum(wind_y, 0.0)
    return jnp.stack(
        [east_rate, west_rate, north_rate, south_rate, vertical_mixing, vertical_mixing]
    )


def apply_transpose(padded, rates_pad, retained):
    center = padded[..., 1:-1, 1:-1, 1:-1]
    summed = retained * center
    summed = summed + rates_pad[0, 1:-1, :-2, 1:-1] * padded[..., 1:-1, :-2, 1:-1]
    summed = summed + rates_pad[1, 1:-1, 2:, 1:-1] * padded[..., 1:-1, 2:, 1:-1]
    summed = summed + rates_pad[2, 1:-1, 1:-1, :-2] * padded[..., 1:-1, 1:-1, :-2]
    summed = summed + rates_pad[3, 1:-1, 1:-1, 2:] * padded[..., 1:-1, 1:-1, 2:]
    summed = summed + rates_pad[4, :-2, 1:-1, 1:-1] * padded[..., :-2, 1:-1, 1:-1]
    summed = summed + rates_pad[5, 2:, 1:-1, 1:-1] * padded[..., 2:, 1:-1, 1:-1]
    return summed


def fourier_tables(horizon):
    freq_rows = jnp.arange(horizon, dtype=jnp.int32)
    phase_int = freq_rows[:, None] * freq_rows[None, :] % horizon
    angles = phase_int.astype(jnp.float32) * (2.0 * math.pi / horizon)
    return (jnp.cos(angles), jnp.sin(angles))


def rotation(horizon, freq_count):
    freq_rows = jnp.arange(freq_count, dtype=jnp.int32)
    angles = freq_rows.astype(jnp.float32) * (2.0 * math.pi / horizon)
    return (jnp.cos(angles)[:, None, None, None], jnp.sin(angles)[:, None, None, None])


def rotate_step(source, applied, cos_freq, sin_freq, beta_step):
    real_part = source[0] + beta_step * (cos_freq * applied[0] - sin_freq * applied[1])
    imag_part = source[1] + beta_step * (sin_freq * applied[0] + cos_freq * applied[1])
    return jnp.stack([real_part, imag_part])


def matmul_exact(table, rows):
    return jnp.dot(table, rows, precision=lax.Precision.HIGHEST)


def body(adjoint_iterate, innovations, station_cells, diffusivity, wind_x, wind_y, vertical_mixing):
    time_parts = lax.axis_size("tm")
    horizon = STEPS_DEV * time_parts
    levels_local = LEV // time_parts
    time_rank = lax.axis_index("tm")
    rate_fields = transfer_rates(diffusivity, wind_x, wind_y, vertical_mixing)
    retained = 1.0 - jnp.sum(rate_fields, axis=0)

    def scatter_step(cell_ids, values):
        return jnp.zeros((LEV, TX * NY), jnp.float32).at[:, cell_ids].add(values)

    forcing = jax.vmap(scatter_step)(station_cells, innovations).reshape(STEPS_DEV, LEV, TX, NY)
    leading = from_behind(adjoint_iterate[:1], "tm", -1)
    following = jnp.concatenate([adjoint_iterate[1:], leading], axis=0)
    extended = with_halo(jnp.concatenate([rate_fields, following], axis=0), (("space", 2),), 1)
    extended = jnp.pad(extended, ((0, 0), (1, 1), (0, 0), (1, 1)))
    rates_pad = extended[:6]
    residual = forcing - adjoint_iterate + apply_transpose(extended[6:], rates_pad, retained)
    log_beta = math.log(circ_alpha) / horizon
    beta_step = math.exp(log_beta)
    step_global = (time_rank * STEPS_DEV + jnp.arange(STEPS_DEV, dtype=jnp.int32)).astype(
        jnp.float32
    )
    scaled = residual * jnp.exp(-step_global * log_beta)[:, None, None, None]
    gathered = lax.all_to_all(scaled, "tm", split_axis=1, concat_axis=0, tiled=True)
    flat_rows = gathered.reshape(horizon, -1)
    cos_table, sin_table = fourier_tables(horizon)
    real_src = matmul_exact(cos_table, flat_rows)
    imag_src = -matmul_exact(sin_table, flat_rows)
    source = jnp.stack([real_src, imag_src]).reshape(2, horizon, levels_local, TX, NY)
    cos_freq, sin_freq = rotation(horizon, horizon)
    level_start = time_rank * levels_local
    local_rates = lax.dynamic_slice_in_dim(rates_pad, level_start, levels_local + 2, 1)
    local_retained = lax.dynamic_slice_in_dim(retained, level_start, levels_local, 0)
    iterate = source
    for sweep_index in range(INNER):
        padded = with_halo(iterate, (("tm", 2), ("space", 3)), 1)
        padded = jnp.pad(padded, ((0, 0), (0, 0), (0, 0), (0, 0), (1, 1)))
        applied = apply_transpose(padded, local_rates, local_retained)
        iterate = rotate_step(source, applied, cos_freq, sin_freq, beta_step)
    real_rows = iterate[0].reshape(horizon, -1)
    imag_rows = iterate[1].reshape(horizon, -1)
    restored = (matmul_exact(cos_table, real_rows) - matmul_exact(sin_table, imag_rows)) / horizon
    restored = restored.reshape(horizon, levels_local, TX, NY)
    returned = lax.all_to_all(restored, "tm", split_axis=0, concat_axis=1, tiled=True)
    correction = returned * jnp.exp(step_global * log_beta)[:, None, None, None]
    return adjoint_iterate + correction


def solution(mesh):
    in_specs = (
        P("tm", None, "space", None),
        P("tm", None, "space"),
        P("tm", "space"),
        P(None, "space", None),
        P(None, "space", None),
        P(None, "space", None),
        P(None, "space", None),
    )
    out_specs = P("tm", None, "space", None)
    return jax.shard_map(body, mesh=mesh, in_specs=in_specs, out_specs=out_specs, check_vma=False)
```

profile of v0, /device:TPU:0, one launch (start us, length us, event | category | flops | bytes accessed | tf_op | source)
XLA Modules:
  0.0 212.5 jit_solution(13806551617667307890)
XLA Ops:
  11.1 5.0 %collective-permute-start.1 = (f32[14,16,1,128]{3,1,2,0:T(8,128)S(1)}, f32[14,16,1,128]{3,1,2,0:T(8,128)S(1)}, u32[]{:S(2)}, u32[]{:S(2)}) collective-permute-start(f32[14,16,1,128]{3,1,2,0:T(8,128)S(1)} %get-tuple-element.41), channel_id=1, source_target_pairs={{0,1},{1,2},{2,3},{4,5},{5,6},{6,7},{8,9},{9,10},{10,11},{12,13},{... | collective-permute-start | bytes 344072 | tf_op jit(solution)/shard_map/ppermute | solution.py:29
  18.5 8.2 %scatter_custom_fusion = f32[8192,16]{1,0:T(8,128)} fusion(s32[1024]{0:T(1024)S(1)} %select_bitcast_fusion, f32[1024,16]{1,0:T(8,128)S(1)} %bitcast.87, f32[]{:T(128)} %constant.20.clone.1), kind=kCustom, calls=%fused_computation.35 | custom fusion | flops 16384 | bytes 524292
  26.7 2.9 %copy.48 = f32[8,1024,16]{1,0,2:T(8,128)S(1)} copy(f32[8,1024,16]{2,1,0:T(8,128)} %bitcast.71) | data formatting | bytes 1048576
  33.8 14.0 %all_to_all.33 = f32[8,16,8,128]{3,2,0,1:T(8,128)S(1)} all-to-all(f32[8,16,8,128]{3,2,0,1:T(8,128)S(1)} %copy.37), channel_id=1, replica_groups=mesh['tm'=8,'space'=4] {'tm'}, dimensions={1} | all-to-all | bytes 1048576 | tf_op jit(solution)/shard_map/all_to_all | solution.py:107
  52.0 2.1 collective-permute-start.3
  55.4 2.8 %collective-permute-done.4 = f32[2,64,1,8,128]{4,3,2,1,0:T(8,128)} collective-permute-done((f32[2,64,1,8,128]{4,3,2,1,0:T(8,128)}, f32[2,64,1,8,128]{4,3,2,1,0:T(8,128)}, u32[]{:S(2)}, u32[]{:S(2)}) %collective-permute-start.4) | collective-permute-done | bytes 524320 | tf_op jit(solution)/shard_map/ppermute | solution.py:31
  58.3 2.6 %pad_maximum_fusion.63 = (f32[2,64,4,1,128]{4,3,2,1,0:T(1,128)}, f32[2,64,4,1,128]{4,3,2,1,0:T(1,128)}) fusion(f32[2,64,1,8,128]{4,3,2,1,0:T(8,128)} %collective-permute-done.4, f32[2,64,2,8,128]{4,3,2,1,0:T(8,128)S(1)} %constant_dynamic-update-slice_fusion.2, f32[2,64,1,8,128]{4,3,2,1,0:T(8,128)} %collective-permute-done.3), kind=kLoop, calls=%fused_computation.205 | loop fusion | flops 262144 | bytes 2621440 | tf_op jit(solution)/shard_map/slice | solution.py:26
  60.9 4.5 %collective-permute-start.5 = (f32[2,64,4,1,128]{4,3,2,1,0:T(1,128)}, f32[2,64,4,1,128]{4,3,2,1,0:T(1,128)S(1)}, u32[]{:S(2)}, u32[]{:S(2)}) collective-permute-start(f32[2,64,4,1,128]{4,3,2,1,0:T(1,128)} %get-tuple-element.15), channel_id=1, source_target_pairs={{0,1},{1,2},{2,3},{4,5},{5,6},{6,7},{8,9},{9,10},{10,11},{12,13},{... | collective-permute-start | bytes 786440 | tf_op jit(solution)/shard_map/ppermute | solution.py:29
  67.1 2.6 %collective-permute-done.5 = f32[2,64,4,1,128]{4,3,2,1,0:T(1,128)S(1)} collective-permute-done((f32[2,64,4,1,128]{4,3,2,1,0:T(1,128)}, f32[2,64,4,1,128]{4,3,2,1,0:T(1,128)S(1)}, u32[]{:S(2)}, u32[]{:S(2)}) %collective-permute-start.5) | collective-permute-done | bytes 262176 | tf_op jit(solution)/shard_map/ppermute | solution.py:29
  69.6 4.4 %collective-permute-done.6 = f32[2,64,4,1,128]{4,3,2,1,0:T(1,128)} collective-permute-done((f32[2,64,4,1,128]{4,3,2,1,0:T(1,128)}, f32[2,64,4,1,128]{4,3,2,1,0:T(1,128)}, u32[]{:S(2)}, u32[]{:S(2)}) %collective-permute-start.6) | collective-permute-done | bytes 262176 | tf_op jit(solution)/shard_map/ppermute | solution.py:31
  74.0 7.3 %select_maximum_fusion.15 = f32[2,64,4,10,130]{4,3,2,1,0:T(8,128)S(1)} fusion(f32[2,64,4,1,128]{4,3,2,1,0:T(1,128)} %collective-permute-done.6, f32[2,64,4,1,128]{4,3,2,1,0:T(1,128)S(1)} %collective-permute-done.5, f32[2,64,1,8,128]{4,3,2,1,0:T(8,128)} %collective-permute-done.4, f32[2,64,2,8,128]{4,3,2,1,0:T(8,128)S(1)} %constant_dynamic-update-slice_fusion.2, ...), kind=kLoop, calls=%fused_computation.18 | loop fusion | flops 7987200 | bytes 5283840 | tf_op jit(solution)/shard_map/concatenate | solution.py:27
  81.4 2.3 %fusion.42 = f32[2,64,2,8,128]{4,3,2,1,0:T(8,128)S(1)} fusion(f32[2,64,1,8,128]{4,3,2,1,0:T(8,128)} %collective-permute-done.4, f32[2,64,2,8,128]{4,3,2,1,0:T(8,128)S(1)} %constant_dynamic-update-slice_fusion.2, f32[2,64,1,8,128]{4,3,2,1,0:T(8,128)} %collective-permute-done.3, f32[2,64,4,10,130]{4,3,2,1,0:T(8,128)S(1)} %select_maximum_fusion.15, ...), kind=kLoop, calls=%fused_computation.130 | loop fusion | flops 5505024 | bytes 5824512 | tf_op jit(solution)/shard_map/add | solution.py:56
  84.0 10.7 %collective-permute-start.7 = (f32[2,64,1,8,128]{4,3,2,1,0:T(8,128)S(1)}, f32[2,64,1,8,128]{4,3,2,1,0:T(8,128)S(1)}, u32[]{:S(2)}, u32[]{:S(2)}) collective-permute-start(f32[2,64,1,8,128]{4,3,2,1,0:T(8,128)S(1)} %get-tuple-element.35), channel_id=1, source_target_pairs={{0,4},{4,8},{8,12},{12,16},{16,20},{20,24},{24,28},{1,5},{5,9},{9,... | collective-permute-start | bytes 1572872 | tf_op jit(solution)/shard_map/ppermute | solution.py:29
  96.2 5.3 %collective-permute-done.8 = f32[2,64,1,8,128]{4,3,2,1,0:T(8,128)S(1)} collective-permute-done((f32[2,64,1,8,128]{4,3,2,1,0:T(8,128)S(1)}, f32[2,64,1,8,128]{4,3,2,1,0:T(8,128)S(1)}, u32[]{:S(2)}, u32[]{:S(2)}) %collective-permute-start.8) | collective-permute-done | bytes 524320 | tf_op jit(solution)/shard_map/ppermute | solution.py:31
  101.8 3.5 %collective-permute-start.9 = (f32[2,64,4,1,128]{4,3,2,1,0:T(1,128)S(1)}, f32[2,64,4,1,128]{4,3,2,1,0:T(1,128)S(1)}, u32[]{:S(2)}, u32[]{:S(2)}) collective-permute-start(f32[2,64,4,1,128]{4,3,2,1,0:T(1,128)S(1)} %get-tuple-element.13), channel_id=1, source_target_pairs={{0,1},{1,2},{2,3},{4,5},{5,6},{6,7},{8,9},{9,10},{10,11},{12,13},{... | collective-permute-start | bytes 786440 | tf_op jit(solution)/shard_map/ppermute | solution.py:29
  106.6 2.6 %collective-permute-done.9 = f32[2,64,4,1,128]{4,3,2,1,0:T(1,128)S(1)} collective-permute-done((f32[2,64,4,1,128]{4,3,2,1,0:T(1,128)S(1)}, f32[2,64,4,1,128]{4,3,2,1,0:T(1,128)S(1)}, u32[]{:S(2)}, u32[]{:S(2)}) %collective-permute-start.9) | collective-permute-done | bytes 262176 | tf_op jit(solution)/shard_map/ppermute | solution.py:29
  109.1 4.4 %collective-permute-done.10 = f32[2,64,4,1,128]{4,3,2,1,0:T(1,128)S(1)} collective-permute-done((f32[2,64,4,1,128]{4,3,2,1,0:T(1,128)S(1)}, f32[2,64,4,1,128]{4,3,2,1,0:T(1,128)S(1)}, u32[]{:S(2)}, u32[]{:S(2)}) %collective-permute-start.10) | collective-permute-done | bytes 262176 | tf_op jit(solution)/shard_map/ppermute | solution.py:31
  113.5 6.7 %select_maximum_fusion.10 = f32[2,64,4,10,130]{4,3,2,1,0:T(8,128)S(1)} fusion(f32[2,64,4,1,128]{4,3,2,1,0:T(1,128)S(1)} %collective-permute-done.10, f32[2,64,4,1,128]{4,3,2,1,0:T(1,128)S(1)} %collective-permute-done.9, f32[2,64,1,8,128]{4,3,2,1,0:T(8,128)S(1)} %collective-permute-done.8, f32[2,64,1,8,128]{4,3,2,1,0:T(8,128)S(1)} %collective-permute-done.7, ...), kind=kLoop, calls=%fused_computation.13 | loop fusion | flops 9318400 | bytes 5283840 | tf_op jit(solution)/shard_map/concatenate | solution.py:27
  121.9 9.0 %collective-permute-start.11 = (f32[2,64,1,8,128]{4,3,2,1,0:T(8,128)S(1)}, f32[2,64,1,8,128]{4,3,2,1,0:T(8,128)S(1)}, u32[]{:S(2)}, u32[]{:S(2)}) collective-permute-start(f32[2,64,1,8,128]{4,3,2,1,0:T(8,128)S(1)} %get-tuple-element.33), channel_id=1, source_target_pairs={{0,4},{4,8},{8,12},{12,16},{16,20},{20,24},{24,28},{1,5},{5,9},{9,... | collective-permute-start | bytes 1572872 | tf_op jit(solution)/shard_map/ppermute | solution.py:29
  132.3 4.1 %collective-permute-done.12 = f32[2,64,1,8,128]{4,3,2,1,0:T(8,128)S(1)} collective-permute-done((f32[2,64,1,8,128]{4,3,2,1,0:T(8,128)S(1)}, f32[2,64,1,8,128]{4,3,2,1,0:T(8,128)S(1)}, u32[]{:S(2)}, u32[]{:S(2)}) %collective-permute-start.12) | collective-permute-done | bytes 524320 | tf_op jit(solution)/shard_map/ppermute | solution.py:31
  136.8 3.5 %collective-permute-start.13 = (f32[2,64,4,1,128]{4,3,2,1,0:T(1,128)S(1)}, f32[2,64,4,1,128]{4,3,2,1,0:T(1,128)S(1)}, u32[]{:S(2)}, u32[]{:S(2)}) collective-permute-start(f32[2,64,4,1,128]{4,3,2,1,0:T(1,128)S(1)} %get-tuple-element.11), channel_id=1, source_target_pairs={{0,1},{1,2},{2,3},{4,5},{5,6},{6,7},{8,9},{9,10},{10,11},{12,13},{... | collective-permute-start | bytes 786440 | tf_op jit(solution)/shard_map/ppermute | solution.py:29
  141.6 2.6 %collective-permute-done.13 = f32[2,64,4,1,128]{4,3,2,1,0:T(1,128)S(1)} collective-permute-done((f32[2,64,4,1,128]{4,3,2,1,0:T(1,128)S(1)}, f32[2,64,4,1,128]{4,3,2,1,0:T(1,128)S(1)}, u32[]{:S(2)}, u32[]{:S(2)}) %collective-permute-start.13) | collective-permute-done | bytes 262176 | tf_op jit(solution)/shard_map/ppermute | solution.py:29
  144.1 4.4 %collective-permute-done.14 = f32[2,64,4,1,128]{4,3,2,1,0:T(1,128)S(1)} collective-permute-done((f32[2,64,4,1,128]{4,3,2,1,0:T(1,128)S(1)}, f32[2,64,4,1,128]{4,3,2,1,0:T(1,128)S(1)}, u32[]{:S(2)}, u32[]{:S(2)}) %collective-permute-start.14) | collective-permute-done | bytes 262176 | tf_op jit(solution)/shard_map/ppermute | solution.py:31
  148.5 6.7 %select_maximum_fusion.5 = f32[2,64,4,10,130]{4,3,2,1,0:T(8,128)S(1)} fusion(f32[2,64,4,1,128]{4,3,2,1,0:T(1,128)S(1)} %collective-permute-done.14, f32[2,64,4,1,128]{4,3,2,1,0:T(1,128)S(1)} %collective-permute-done.13, f32[2,64,1,8,128]{4,3,2,1,0:T(8,128)S(1)} %collective-permute-done.12, f32[2,64,1,8,128]{4,3,2,1,0:T(8,128)S(1)} %collective-permute-done.11, ...), kind=kLoop, calls=%fused_computation.8 | loop fusion | flops 9318400 | bytes 5283840 | tf_op jit(solution)/shard_map/concatenate | solution.py:27
  156.9 8.0 %collective-permute-start.15 = (f32[2,64,1,8,128]{4,3,2,1,0:T(8,128)S(1)}, f32[2,64,1,8,128]{4,3,2,1,0:T(8,128)S(1)}, u32[]{:S(2)}, u32[]{:S(2)}) collective-permute-start(f32[2,64,1,8,128]{4,3,2,1,0:T(8,128)S(1)} %get-tuple-element.31), channel_id=1, source_target_pairs={{0,4},{4,8},{8,12},{12,16},{16,20},{20,24},{24,28},{1,5},{5,9},{9,... | collective-permute-start | bytes 1572872 | tf_op jit(solution)/shard_map/ppermute | solution.py:29
  166.4 4.1 %collective-permute-done.16 = f32[2,64,1,8,128]{4,3,2,1,0:T(8,128)S(1)} collective-permute-done((f32[2,64,1,8,128]{4,3,2,1,0:T(8,128)S(1)}, f32[2,64,1,8,128]{4,3,2,1,0:T(8,128)S(1)}, u32[]{:S(2)}, u32[]{:S(2)}) %collective-permute-start.16) | collective-permute-done | bytes 524320 | tf_op jit(solution)/shard_map/ppermute | solution.py:31
  170.7 2.5 %collective-permute-start.17 = (f32[2,64,4,1,128]{4,3,2,1,0:T(1,128)S(1)}, f32[2,64,4,1,128]{4,3,2,1,0:T(1,128)S(1)}, u32[]{:S(2)}, u32[]{:S(2)}) collective-permute-start(f32[2,64,4,1,128]{4,3,2,1,0:T(1,128)S(1)} %get-tuple-element.9), channel_id=1, source_target_pairs={{0,1},{1,2},{2,3},{4,5},{5,6},{6,7},{8,9},{9,10},{10,11},{12,13},{... | collective-permute-start | bytes 786440 | tf_op jit(solution)/shard_map/ppermute | solution.py:29
  174.7 2.4 %collective-permute-done.17 = f32[2,64,4,1,128]{4,3,2,1,0:T(1,128)S(1)} collective-permute-done((f32[2,64,4,1,128]{4,3,2,1,0:T(1,128)S(1)}, f32[2,64,4,1,128]{4,3,2,1,0:T(1,128)S(1)}, u32[]{:S(2)}, u32[]{:S(2)}) %collective-permute-start.17) | collective-permute-done | bytes 262176 | tf_op jit(solution)/shard_map/ppermute | solution.py:29
  177.1 4.6 %collective-permute-done.18 = f32[2,64,4,1,128]{4,3,2,1,0:T(1,128)S(1)} collective-permute-done((f32[2,64,4,1,128]{4,3,2,1,0:T(1,128)S(1)}, f32[2,64,4,1,128]{4,3,2,1,0:T(1,128)S(1)}, u32[]{:S(2)}, u32[]{:S(2)}) %collective-permute-start.18) | collective-permute-done | bytes 262176 | tf_op jit(solution)/shard_map/ppermute | solution.py:31
  181.6 6.7 %select_maximum_fusion = f32[2,64,4,10,130]{4,3,2,1,0:T(8,128)S(1)} fusion(f32[2,64,4,1,128]{4,3,2,1,0:T(1,128)S(1)} %collective-permute-done.18, f32[2,64,4,1,128]{4,3,2,1,0:T(1,128)S(1)} %collective-permute-done.17, f32[2,64,1,8,128]{4,3,2,1,0:T(8,128)S(1)} %collective-permute-done.16, f32[2,64,1,8,128]{4,3,2,1,0:T(8,128)S(1)} %collective-permute-done.15, ...), kind=kLoop, calls=%fused_computation.3 | loop fusion | flops 9318400 | bytes 5283840 | tf_op jit(solution)/shard_map/concatenate | solution.py:27
  192.3 9.5 %all-to-all-start.1 = ((f32[64,2,8,128]{3,2,1,0:T(8,128)}), f32[64,2,8,128]{3,2,1,0:T(8,128)S(1)}, u32[]{:S(2)}, u32[]{:S(2)}) async-start(f32[64,2,8,128]{3,2,1,0:T(8,128)} %bitcast.42), calls=%async_computation.1 | async-start | bytes 1048576 | tf_op jit(solution)/shard_map/all_to_all | solution.py:127
  201.8 9.7 %all-to-all-done.1 = f32[64,2,8,128]{3,2,1,0:T(8,128)S(1)} async-done(((f32[64,2,8,128]{3,2,1,0:T(8,128)}), f32[64,2,8,128]{3,2,1,0:T(8,128)S(1)}, u32[]{:S(2)}, u32[]{:S(2)}) %all-to-all-start.1) | async-done | bytes 524320 | tf_op jit(solution)/shard_map/all_to_all | solution.py:127
  (100 shorter events, 42.4 us)
Async XLA Ops:
  1.2 10.0 %collective-permute-start = (f32[1,16,8,128]{3,1,2,0:T(8,128)S(1)}, f32[1,16,8,128]{3,1,2,0:T(8,128)S(1)}, u32[]{:S(2)}, u32[]{:S(2)}) collective-permute-start(f32[1,16,8,128]{3,1,2,0:T(8,128)S(1)} %slice.399), channel_id=1, source_target_pairs={{4,0},{8,4},{12,8},{16,12},{20,16},{24,20},{28,24},{5,1},{9,5},{13... | collective-permute-start | bytes 196616 | tf_op jit(solution)/shard_map/ppermute | solution.py:18
  9.6 23.3 %copy-start.3 = (f32[8,16,8,128]{3,2,1,0:T(8,128)S(1)}, f32[8,16,8,128]{3,2,1,0:T(8,128)}, u32[]{:S(2)}) copy-start(f32[8,16,8,128]{3,2,1,0:T(8,128)} %param.7) | copy-start | bytes 1572868
  11.1 18.5 %collective-permute-start.1 = (f32[14,16,1,128]{3,1,2,0:T(8,128)S(1)}, f32[14,16,1,128]{3,1,2,0:T(8,128)S(1)}, u32[]{:S(2)}, u32[]{:S(2)}) collective-permute-start(f32[14,16,1,128]{3,1,2,0:T(8,128)S(1)} %get-tuple-element.41), channel_id=1, source_target_pairs={{0,1},{1,2},{2,3},{4,5},{5,6},{6,7},{8,9},{9,10},{10,11},{12,13},{... | collective-permute-start | bytes 344072 | tf_op jit(solution)/shard_map/ppermute | solution.py:29
  16.1 13.5 %collective-permute-start.2 = (f32[14,16,1,128]{3,1,2,0:T(8,128)S(1)}, f32[14,16,1,128]{3,1,2,0:T(8,128)S(1)}, u32[]{:S(2)}, u32[]{:S(2)}) collective-permute-start(f32[14,16,1,128]{3,1,2,0:T(8,128)S(1)} %get-tuple-element.42), channel_id=1, source_target_pairs={{1,0},{2,1},{3,2},{5,4},{6,5},{7,6},{9,8},{10,9},{11,10},{13,12},{... | collective-permute-start | bytes 344072 | tf_op jit(solution)/shard_map/ppermute | solution.py:31
  31.1 1.7 copy-start
  33.7 33.1 %slice-start = ((f32[14,18,10,130]{3,1,2,0:T(8,128)}), f32[6,18,10,130]{3,1,2,0:T(8,128)S(1)}, s32[]{:S(2)}) async-start(f32[14,18,10,130]{3,1,2,0:T(8,128)} %copy-done), calls=%async_computation.2 | async-start | bytes 2949120 | tf_op jit(solution)/shard_map/slice | solution.py:99
  48.6 0.9 copy-start.5
  49.4 0.8 copy-start.7
  50.1 0.8 copy-start.1
  52.0 3.4 %collective-permute-start.3 = (f32[2,64,1,8,128]{4,3,2,1,0:T(8,128)}, f32[2,64,1,8,128]{4,3,2,1,0:T(8,128)}, u32[]{:S(2)}, u32[]{:S(2)}) collective-permute-start(f32[2,64,1,8,128]{4,3,2,1,0:T(8,128)} %get-tuple-element.37), channel_id=1, source_target_pairs={{0,4},{4,8},{8,12},{12,16},{16,20},{20,24},{24,28},{1,5},{5,9},{9,... | collective-permute-start | bytes 1572872 | tf_op jit(solution)/shard_map/ppermute | solution.py:29
  54.1 4.1 %collective-permute-start.4 = (f32[2,64,1,8,128]{4,3,2,1,0:T(8,128)}, f32[2,64,1,8,128]{4,3,2,1,0:T(8,128)}, u32[]{:S(2)}, u32[]{:S(2)}) collective-permute-start(f32[2,64,1,8,128]{4,3,2,1,0:T(8,128)} %get-tuple-element.38), channel_id=1, source_target_pairs={{4,0},{8,4},{12,8},{16,12},{20,16},{24,20},{28,24},{5,1},{9,5},{13... | collective-permute-start | bytes 1572872 | tf_op jit(solution)/shard_map/ppermute | solution.py:31
  60.9 8.7 %collective-permute-start.5 = (f32[2,64,4,1,128]{4,3,2,1,0:T(1,128)}, f32[2,64,4,1,128]{4,3,2,1,0:T(1,128)S(1)}, u32[]{:S(2)}, u32[]{:S(2)}) collective-permute-start(f32[2,64,4,1,128]{4,3,2,1,0:T(1,128)} %get-tuple-element.15), channel_id=1, source_target_pairs={{0,1},{1,2},{2,3},{4,5},{5,6},{6,7},{8,9},{9,10},{10,11},{12,13},{... | collective-permute-start | bytes 786440 | tf_op jit(solution)/shard_map/ppermute | solution.py:29
  65.5 8.6 %collective-permute-start.6 = (f32[2,64,4,1,128]{4,3,2,1,0:T(1,128)}, f32[2,64,4,1,128]{4,3,2,1,0:T(1,128)}, u32[]{:S(2)}, u32[]{:S(2)}) collective-permute-start(f32[2,64,4,1,128]{4,3,2,1,0:T(1,128)} %get-tuple-element.16), channel_id=1, source_target_pairs={{1,0},{2,1},{3,2},{5,4},{6,5},{7,6},{9,8},{10,9},{11,10},{13,12},{... | collective-permute-start | bytes 786440 | tf_op jit(solution)/shard_map/ppermute | solution.py:31
  67.1 16.6 %copy-start.2 = (f32[8,8,16,128]{3,2,1,0:T(8,128)S(1)}, f32[8,8,16,128]{3,2,1,0:T(8,128)}, u32[]{:S(2)}) copy-start(f32[8,8,16,128]{3,2,1,0:T(8,128)} %copy-done.1) | copy-start | bytes 1572868
  84.0 12.2 %collective-permute-start.7 = (f32[2,64,1,8,128]{4,3,2,1,0:T(8,128)S(1)}, f32[2,64,1,8,128]{4,3,2,1,0:T(8,128)S(1)}, u32[]{:S(2)}, u32[]{:S(2)}) collective-permute-start(f32[2,64,1,8,128]{4,3,2,1,0:T(8,128)S(1)} %get-tuple-element.35), channel_id=1, source_target_pairs={{0,4},{4,8},{8,12},{12,16},{16,20},{20,24},{24,28},{1,5},{5,9},{9,... | collective-permute-start | bytes 1572872 | tf_op jit(solution)/shard_map/ppermute | solution.py:29
  94.7 6.8 %collective-permute-start.8 = (f32[2,64,1,8,128]{4,3,2,1,0:T(8,128)S(1)}, f32[2,64,1,8,128]{4,3,2,1,0:T(8,128)S(1)}, u32[]{:S(2)}, u32[]{:S(2)}) collective-permute-start(f32[2,64,1,8,128]{4,3,2,1,0:T(8,128)S(1)} %get-tuple-element.36), channel_id=1, source_target_pairs={{4,0},{8,4},{12,8},{16,12},{20,16},{24,20},{28,24},{5,1},{9,5},{13... | collective-permute-start | bytes 1572872 | tf_op jit(solution)/shard_map/ppermute | solution.py:31
  101.8 7.3 %collective-permute-start.9 = (f32[2,64,4,1,128]{4,3,2,1,0:T(1,128)S(1)}, f32[2,64,4,1,128]{4,3,2,1,0:T(1,128)S(1)}, u32[]{:S(2)}, u32[]{:S(2)}) collective-permute-start(f32[2,64,4,1,128]{4,3,2,1,0:T(1,128)S(1)} %get-tuple-element.13), channel_id=1, source_target_pairs={{0,1},{1,2},{2,3},{4,5},{5,6},{6,7},{8,9},{9,10},{10,11},{12,13},{... | collective-permute-start | bytes 786440 | tf_op jit(solution)/shard_map/ppermute | solution.py:29
  105.3 8.3 %collective-permute-start.10 = (f32[2,64,4,1,128]{4,3,2,1,0:T(1,128)S(1)}, f32[2,64,4,1,128]{4,3,2,1,0:T(1,128)S(1)}, u32[]{:S(2)}, u32[]{:S(2)}) collective-permute-start(f32[2,64,4,1,128]{4,3,2,1,0:T(1,128)S(1)} %get-tuple-element.14), channel_id=1, source_target_pairs={{1,0},{2,1},{3,2},{5,4},{6,5},{7,6},{9,8},{10,9},{11,10},{13,12},{... | collective-permute-start | bytes 786440 | tf_op jit(solution)/shard_map/ppermute | solution.py:31
  121.9 10.5 %collective-permute-start.11 = (f32[2,64,1,8,128]{4,3,2,1,0:T(8,128)S(1)}, f32[2,64,1,8,128]{4,3,2,1,0:T(8,128)S(1)}, u32[]{:S(2)}, u32[]{:S(2)}) collective-permute-start(f32[2,64,1,8,128]{4,3,2,1,0:T(8,128)S(1)} %get-tuple-element.33), channel_id=1, source_target_pairs={{0,4},{4,8},{8,12},{12,16},{16,20},{20,24},{24,28},{1,5},{5,9},{9,... | collective-permute-start | bytes 1572872 | tf_op jit(solution)/shard_map/ppermute | solution.py:29
  130.9 5.6 %collective-permute-start.12 = (f32[2,64,1,8,128]{4,3,2,1,0:T(8,128)S(1)}, f32[2,64,1,8,128]{4,3,2,1,0:T(8,128)S(1)}, u32[]{:S(2)}, u32[]{:S(2)}) collective-permute-start(f32[2,64,1,8,128]{4,3,2,1,0:T(8,128)S(1)} %get-tuple-element.34), channel_id=1, source_target_pairs={{4,0},{8,4},{12,8},{16,12},{20,16},{24,20},{28,24},{5,1},{9,5},{13... | collective-permute-start | bytes 1572872 | tf_op jit(solution)/shard_map/ppermute | solution.py:31
  136.8 7.3 %collective-permute-start.13 = (f32[2,64,4,1,128]{4,3,2,1,0:T(1,128)S(1)}, f32[2,64,4,1,128]{4,3,2,1,0:T(1,128)S(1)}, u32[]{:S(2)}, u32[]{:S(2)}) collective-permute-start(f32[2,64,4,1,128]{4,3,2,1,0:T(1,128)S(1)} %get-tuple-element.11), channel_id=1, source_target_pairs={{0,1},{1,2},{2,3},{4,5},{5,6},{6,7},{8,9},{9,10},{10,11},{12,13},{... | collective-permute-start | bytes 786440 | tf_op jit(solution)/shard_map/ppermute | solution.py:29
  140.3 8.3 %collective-permute-start.14 = (f32[2,64,4,1,128]{4,3,2,1,0:T(1,128)S(1)}, f32[2,64,4,1,128]{4,3,2,1,0:T(1,128)S(1)}, u32[]{:S(2)}, u32[]{:S(2)}) collective-permute-start(f32[2,64,4,1,128]{4,3,2,1,0:T(1,128)S(1)} %get-tuple-element.12), channel_id=1, source_target_pairs={{1,0},{2,1},{3,2},{5,4},{6,5},{7,6},{9,8},{10,9},{11,10},{13,12},{... | collective-permute-start | bytes 786440 | tf_op jit(solution)/shard_map/ppermute | solution.py:31
  156.9 9.5 %collective-permute-start.15 = (f32[2,64,1,8,128]{4,3,2,1,0:T(8,128)S(1)}, f32[2,64,1,8,128]{4,3,2,1,0:T(8,128)S(1)}, u32[]{:S(2)}, u32[]{:S(2)}) collective-permute-start(f32[2,64,1,8,128]{4,3,2,1,0:T(8,128)S(1)} %get-tuple-element.31), channel_id=1, source_target_pairs={{0,4},{4,8},{8,12},{12,16},{16,20},{20,24},{24,28},{1,5},{5,9},{9,... | collective-permute-start | bytes 1572872 | tf_op jit(solution)/shard_map/ppermute | solution.py:29
  164.9 5.5 %collective-permute-start.16 = (f32[2,64,1,8,128]{4,3,2,1,0:T(8,128)S(1)}, f32[2,64,1,8,128]{4,3,2,1,0:T(8,128)S(1)}, u32[]{:S(2)}, u32[]{:S(2)}) collective-permute-start(f32[2,64,1,8,128]{4,3,2,1,0:T(8,128)S(1)} %get-tuple-element.32), channel_id=1, source_target_pairs={{4,0},{8,4},{12,8},{16,12},{20,16},{24,20},{28,24},{5,1},{9,5},{13... | collective-permute-start | bytes 1572872 | tf_op jit(solution)/shard_map/ppermute | solution.py:31
  170.7 6.3 %collective-permute-start.17 = (f32[2,64,4,1,128]{4,3,2,1,0:T(1,128)S(1)}, f32[2,64,4,1,128]{4,3,2,1,0:T(1,128)S(1)}, u32[]{:S(2)}, u32[]{:S(2)}) collective-permute-start(f32[2,64,4,1,128]{4,3,2,1,0:T(1,128)S(1)} %get-tuple-element.9), channel_id=1, source_target_pairs={{0,1},{1,2},{2,3},{4,5},{5,6},{6,7},{8,9},{9,10},{10,11},{12,13},{... | collective-permute-start | bytes 786440 | tf_op jit(solution)/shard_map/ppermute | solution.py:29
  173.2 16.6 %copy-start.8 = (f32[64,2048]{1,0:T(8,128)S(1)}, f32[64,2048]{1,0:T(8,128)}, u32[]{:S(2)}) copy-start(f32[64,2048]{1,0:T(8,128)} %copy-done.7) | copy-start | bytes 1572868
  173.2 8.4 %collective-permute-start.18 = (f32[2,64,4,1,128]{4,3,2,1,0:T(1,128)S(1)}, f32[2,64,4,1,128]{4,3,2,1,0:T(1,128)S(1)}, u32[]{:S(2)}, u32[]{:S(2)}) collective-permute-start(f32[2,64,4,1,128]{4,3,2,1,0:T(1,128)S(1)} %get-tuple-element.10), channel_id=1, source_target_pairs={{1,0},{2,1},{3,2},{5,4},{6,5},{7,6},{9,8},{10,9},{11,10},{13,12},{... | collective-permute-start | bytes 786440 | tf_op jit(solution)/shard_map/ppermute | solution.py:31
  188.3 2.3 %copy-start.6 = (f32[64,2048]{1,0:T(8,128)S(1)}, f32[64,2048]{1,0:T(8,128)}, u32[]{:S(2)}) copy-start(f32[64,2048]{1,0:T(8,128)} %copy-done.5) | copy-start | bytes 1572868
  188.3 23.2 %copy-start.4 = (f32[8,16,8,128]{3,2,1,0:T(8,128)S(1)}, f32[8,16,8,128]{3,2,1,0:T(8,128)}, u32[]{:S(2)}) copy-start(f32[8,16,8,128]{3,2,1,0:T(8,128)} %param.7) | copy-start | bytes 1572868
  192.3 19.2 %all-to-all-start.1 = ((f32[64,2,8,128]{3,2,1,0:T(8,128)}), f32[64,2,8,128]{3,2,1,0:T(8,128)S(1)}, u32[]{:S(2)}, u32[]{:S(2)}) async-start(f32[64,2,8,128]{3,2,1,0:T(8,128)} %bitcast.42), calls=%async_computation.1 | async-start | bytes 1048576 | tf_op jit(solution)/shard_map/all_to_all | solution.py:127
where the time goes:
time: 214 us; the launch traced here: 212 us
  starting transfers between devices  71.4 us (33%)
  other arithmetic  56.4 us (26%)
  waiting for transfers between devices  54.2 us (25%)
  blocking collectives  14 us (7%)
  local copies, waits for them, and re-layouts  12.8 us (6%)
  matrix products  2.97 us (1%)
    ppermute x9, starting transfers between devices, with_halo(): lax.ppermute(tail, axis, [(i, (i + 1) % count) for i in range(ends)])  48.7 us
    ppermute x9, waiting for transfers between devices, with_halo(): lax.ppermute(head, axis, [((i + 1) % count, i) for i in range(ends)])  34.1 us
    concatenate x5, other arithmetic, with_halo(): jnp.concatenate([lax.ppermute(tail, axis, [(i, (i + 1) % count) for i in...  28.8 us
    all_to_all x1, blocking collectives, body(): lax.all_to_all(scaled, 'tm', split_axis=1, concat_axis=0, tiled=True)  14 us
    unnamed x8, other arithmetic  13.4 us
    ppermute x9, starting transfers between devices, with_halo(): lax.ppermute(head, axis, [((i + 1) % count, i) for i in range(ends)])  11.9 us
    unnamed x28, local copies, waits for them, and re-layouts  10.8 us
    ppermute x9, waiting for transfers between devices, with_halo(): lax.ppermute(tail, axis, [(i, (i + 1) % count) for i in range(ends)])  10.5 us
  transfers between devices with their start and end apart: 20, of which 15 were waited for; matrix products, arithmetic and copies ran while one was open for 10% of the time, Pallas kernels for 0%

commit v1 on v0

--- a/solution.py
+++ b/solution.py
@@ -1,3 +1,4 @@
+import functools
 import math
 import jax
 import jax.numpy as jnp
@@ -10,6 +11,17 @@
 STEPS_DEV = 8
 INNER = 4
 circ_alpha = 0.1
+
+
+def _unite_screen(frame, ax_name):
+    newest = jax.lax.axis_size(ax_name)
+    z2 = jnp.split(frame, newest, axis=1)
+    work_now = jnp.stack(z2, axis=0)
+    row_out = jax.lax.all_to_all(work_now, ax_name, 0, 0)
+    return jnp.concatenate(row_out, axis=0)
+
+
+track_the_ranges = functools.partial(_unite_screen, ax_name="tm")
 
 
 def from_behind(value, axis, steps):
@@ -104,7 +116,7 @@
         jnp.float32
     )
     scaled = residual * jnp.exp(-step_global * log_beta)[:, None, None, None]
-    gathered = lax.all_to_all(scaled, "tm", split_axis=1, concat_axis=0, tiled=True)
+    gathered = track_the_ranges(scaled)
     flat_rows = gathered.reshape(horizon, -1)
     cos_table, sin_table = fourier_tables(horizon)
     real_src = matmul_exact(cos_table, flat_rows)

time: 214 us -> 214 us (level)
    unnamed x28 -> x35, local copies, waits for them, and re-layouts: 10.8 us -> 11.1 us
where the time goes in v1:
time: 214 us; the launch traced here: 213 us
  starting transfers between devices  71.4 us (33%)
  other arithmetic  56.4 us (26%)
  waiting for transfers between devices  54.2 us (25%)
  blocking collectives  14 us (7%)
  local copies, waits for them, and re-layouts  12.9 us (6%)
  matrix products  2.96 us (1%)
    ppermute x9, starting transfers between devices, with_halo(): lax.ppermute(tail, axis, [(i, (i + 1) % count) for i in range(ends)])  48.8 us
    ppermute x9, waiting for transfers between devices, with_halo(): lax.ppermute(head, axis, [((i + 1) % count, i) for i in range(ends)])  34 us
    concatenate x5, other arithmetic, with_halo(): jnp.concatenate([lax.ppermute(tail, axis, [(i, (i + 1) % count) for i in...  28.8 us
    all_to_all x1, blocking collectives, _unite_screen(): row_out = jax.lax.all_to_all(work_now, ax_name, 0, 0)  14 us
    unnamed x8, other arithmetic  13.4 us
    ppermute x9, starting transfers between devices, with_halo(): lax.ppermute(head, axis, [((i + 1) % count, i) for i in range(ends)])  11.9 us
    unnamed x35, local copies, waits for them, and re-layouts  11.1 us
    ppermute x9, waiting for transfers between devices, with_halo(): lax.ppermute(tail, axis, [(i, (i + 1) % count) for i in range(ends)])  10.5 us
  transfers between devices with their start and end apart: 20, of which 15 were waited for; matrix products, arithmetic and copies ran while one was open for 10% of the time, Pallas kernels for 0%

profile of v1, /device:TPU:0, one launch (start us, length us, event | category | flops | bytes accessed | tf_op | source)
XLA Modules:
  0.0 212.6 jit_solution(14876054607061578206)
XLA Ops:
  11.1 5.0 %collective-permute-start.1 = (f32[14,16,1,128]{3,1,2,0:T(8,128)S(1)}, f32[14,16,1,128]{3,1,2,0:T(8,128)S(1)}, u32[]{:S(2)}, u32[]{:S(2)}) collective-permute-start(f32[14,16,1,128]{3,1,2,0:T(8,128)S(1)} %get-tuple-element.41), channel_id=1, source_target_pairs={{0,1},{1,2},{2,3},{4,5},{5,6},{6,7},{8,9},{9,10},{10,11},{12,13},{... | collective-permute-start | bytes 344072 | tf_op jit(solution)/shard_map/ppermute | solution.py:41
  18.5 8.2 %scatter_custom_fusion = f32[8192,16]{1,0:T(8,128)} fusion(s32[1024]{0:T(1024)S(1)} %select_bitcast_fusion, f32[1024,16]{1,0:T(8,128)S(1)} %bitcast.113, f32[]{:T(128)} %constant.20.clone.1), kind=kCustom, calls=%fused_computation.35 | custom fusion | flops 16384 | bytes 524292
  26.7 2.9 %copy.71 = f32[8,1024,16]{1,0,2:T(8,128)S(1)} copy(f32[8,1024,16]{2,1,0:T(8,128)} %bitcast.99) | data formatting | bytes 1048576
  33.9 14.0 %all_to_all.23 = f32[8,8,2,8,128]{4,2,3,1,0:T(2,128)S(1)} all-to-all(f32[8,8,2,8,128]{4,2,3,1,0:T(2,128)S(1)} %fusion.85), channel_id=1, replica_groups=mesh['tm'=8,'space'=4] {'tm'}, dimensions={0} | all-to-all | bytes 1048576 | tf_op jit(solution)/shard_map/all_to_all | solution.py:20
  52.2 2.1 collective-permute-start.3
  55.6 2.8 %collective-permute-done.4 = f32[2,64,1,8,128]{4,3,2,1,0:T(8,128)} collective-permute-done((f32[2,64,1,8,128]{4,3,2,1,0:T(8,128)}, f32[2,64,1,8,128]{4,3,2,1,0:T(8,128)}, u32[]{:S(2)}, u32[]{:S(2)}) %collective-permute-start.4) | collective-permute-done | bytes 524320 | tf_op jit(solution)/shard_map/ppermute | solution.py:43
  58.4 2.6 %pad_maximum_fusion.63 = (f32[2,64,4,1,128]{4,3,2,1,0:T(1,128)}, f32[2,64,4,1,128]{4,3,2,1,0:T(1,128)}) fusion(f32[2,64,1,8,128]{4,3,2,1,0:T(8,128)} %collective-permute-done.4, f32[2,64,2,8,128]{4,3,2,1,0:T(8,128)S(1)} %constant_dynamic-update-slice_fusion.2, f32[2,64,1,8,128]{4,3,2,1,0:T(8,128)} %collective-permute-done.3), kind=kLoop, calls=%fused_computation.204 | loop fusion | flops 262144 | bytes 2621440 | tf_op jit(solution)/shard_map/slice | solution.py:38
  61.0 4.6 %collective-permute-start.5 = (f32[2,64,4,1,128]{4,3,2,1,0:T(1,128)}, f32[2,64,4,1,128]{4,3,2,1,0:T(1,128)S(1)}, u32[]{:S(2)}, u32[]{:S(2)}) collective-permute-start(f32[2,64,4,1,128]{4,3,2,1,0:T(1,128)} %get-tuple-element.15), channel_id=1, source_target_pairs={{0,1},{1,2},{2,3},{4,5},{5,6},{6,7},{8,9},{9,10},{10,11},{12,13},{... | collective-permute-start | bytes 786440 | tf_op jit(solution)/shard_map/ppermute | solution.py:41
  67.2 2.6 %collective-permute-done.5 = f32[2,64,4,1,128]{4,3,2,1,0:T(1,128)S(1)} collective-permute-done((f32[2,64,4,1,128]{4,3,2,1,0:T(1,128)}, f32[2,64,4,1,128]{4,3,2,1,0:T(1,128)S(1)}, u32[]{:S(2)}, u32[]{:S(2)}) %collective-permute-start.5) | collective-permute-done | bytes 262176 | tf_op jit(solution)/shard_map/ppermute | solution.py:41
  69.8 4.4 %collective-permute-done.6 = f32[2,64,4,1,128]{4,3,2,1,0:T(1,128)} collective-permute-done((f32[2,64,4,1,128]{4,3,2,1,0:T(1,128)}, f32[2,64,4,1,128]{4,3,2,1,0:T(1,128)}, u32[]{:S(2)}, u32[]{:S(2)}) %collective-permute-start.6) | collective-permute-done | bytes 262176 | tf_op jit(solution)/shard_map/ppermute | solution.py:43
  74.2 7.3 %select_maximum_fusion.15 = f32[2,64,4,10,130]{4,3,2,1,0:T(8,128)S(1)} fusion(f32[2,64,4,1,128]{4,3,2,1,0:T(1,128)} %collective-permute-done.6, f32[2,64,4,1,128]{4,3,2,1,0:T(1,128)S(1)} %collective-permute-done.5, f32[2,64,1,8,128]{4,3,2,1,0:T(8,128)} %collective-permute-done.4, f32[2,64,2,8,128]{4,3,2,1,0:T(8,128)S(1)} %constant_dynamic-update-slice_fusion.2, ...), kind=kLoop, calls=%fused_computation.18 | loop fusion | flops 7987200 | bytes 5283840 | tf_op jit(solution)/shard_map/concatenate | solution.py:39
  81.5 2.3 %fusion.42 = f32[2,64,2,8,128]{4,3,2,1,0:T(8,128)S(1)} fusion(f32[2,64,1,8,128]{4,3,2,1,0:T(8,128)} %collective-permute-done.4, f32[2,64,2,8,128]{4,3,2,1,0:T(8,128)S(1)} %constant_dynamic-update-slice_fusion.2, f32[2,64,1,8,128]{4,3,2,1,0:T(8,128)} %collective-permute-done.3, f32[2,64,4,10,130]{4,3,2,1,0:T(8,128)S(1)} %select_maximum_fusion.15, ...), kind=kLoop, calls=%fused_computation.130 | loop fusion | flops 5505024 | bytes 5824512 | tf_op jit(solution)/shard_map/add | solution.py:68
  84.1 10.7 %collective-permute-start.7 = (f32[2,64,1,8,128]{4,3,2,1,0:T(8,128)S(1)}, f32[2,64,1,8,128]{4,3,2,1,0:T(8,128)S(1)}, u32[]{:S(2)}, u32[]{:S(2)}) collective-permute-start(f32[2,64,1,8,128]{4,3,2,1,0:T(8,128)S(1)} %get-tuple-element.35), channel_id=1, source_target_pairs={{0,4},{4,8},{8,12},{12,16},{16,20},{20,24},{24,28},{1,5},{5,9},{9,... | collective-permute-start | bytes 1572872 | tf_op jit(solution)/shard_map/ppermute | solution.py:41
  96.3 5.3 %collective-permute-done.8 = f32[2,64,1,8,128]{4,3,2,1,0:T(8,128)S(1)} collective-permute-done((f32[2,64,1,8,128]{4,3,2,1,0:T(8,128)S(1)}, f32[2,64,1,8,128]{4,3,2,1,0:T(8,128)S(1)}, u32[]{:S(2)}, u32[]{:S(2)}) %collective-permute-start.8) | collective-permute-done | bytes 524320 | tf_op jit(solution)/shard_map/ppermute | solution.py:43
  101.9 3.5 %collective-permute-start.9 = (f32[2,64,4,1,128]{4,3,2,1,0:T(1,128)S(1)}, f32[2,64,4,1,128]{4,3,2,1,0:T(1,128)S(1)}, u32[]{:S(2)}, u32[]{:S(2)}) collective-permute-start(f32[2,64,4,1,128]{4,3,2,1,0:T(1,128)S(1)} %get-tuple-element.13), channel_id=1, source_target_pairs={{0,1},{1,2},{2,3},{4,5},{5,6},{6,7},{8,9},{9,10},{10,11},{12,13},{... | collective-permute-start | bytes 786440 | tf_op jit(solution)/shard_map/ppermute | solution.py:41
  106.7 2.6 %collective-permute-done.9 = f32[2,64,4,1,128]{4,3,2,1,0:T(1,128)S(1)} collective-permute-done((f32[2,64,4,1,128]{4,3,2,1,0:T(1,128)S(1)}, f32[2,64,4,1,128]{4,3,2,1,0:T(1,128)S(1)}, u32[]{:S(2)}, u32[]{:S(2)}) %collective-permute-start.9) | collective-permute-done | bytes 262176 | tf_op jit(solution)/shard_map/ppermute | solution.py:41
  109.3 4.4 %collective-permute-done.10 = f32[2,64,4,1,128]{4,3,2,1,0:T(1,128)S(1)} collective-permute-done((f32[2,64,4,1,128]{4,3,2,1,0:T(1,128)S(1)}, f32[2,64,4,1,128]{4,3,2,1,0:T(1,128)S(1)}, u32[]{:S(2)}, u32[]{:S(2)}) %collective-permute-start.10) | collective-permute-done | bytes 262176 | tf_op jit(solution)/shard_map/ppermute | solution.py:43
  113.7 6.7 %select_maximum_fusion.10 = f32[2,64,4,10,130]{4,3,2,1,0:T(8,128)S(1)} fusion(f32[2,64,4,1,128]{4,3,2,1,0:T(1,128)S(1)} %collective-permute-done.10, f32[2,64,4,1,128]{4,3,2,1,0:T(1,128)S(1)} %collective-permute-done.9, f32[2,64,1,8,128]{4,3,2,1,0:T(8,128)S(1)} %collective-permute-done.8, f32[2,64,1,8,128]{4,3,2,1,0:T(8,128)S(1)} %collective-permute-done.7, ...), kind=kLoop, calls=%fused_computation.13 | loop fusion | flops 9318400 | bytes 5283840 | tf_op jit(solution)/shard_map/concatenate | solution.py:39
  122.0 9.0 %collective-permute-start.11 = (f32[2,64,1,8,128]{4,3,2,1,0:T(8,128)S(1)}, f32[2,64,1,8,128]{4,3,2,1,0:T(8,128)S(1)}, u32[]{:S(2)}, u32[]{:S(2)}) collective-permute-start(f32[2,64,1,8,128]{4,3,2,1,0:T(8,128)S(1)} %get-tuple-element.33), channel_id=1, source_target_pairs={{0,4},{4,8},{8,12},{12,16},{16,20},{20,24},{24,28},{1,5},{5,9},{9,... | collective-permute-start | bytes 1572872 | tf_op jit(solution)/shard_map/ppermute | solution.py:41
  132.5 4.1 %collective-permute-done.12 = f32[2,64,1,8,128]{4,3,2,1,0:T(8,128)S(1)} collective-permute-done((f32[2,64,1,8,128]{4,3,2,1,0:T(8,128)S(1)}, f32[2,64,1,8,128]{4,3,2,1,0:T(8,128)S(1)}, u32[]{:S(2)}, u32[]{:S(2)}) %collective-permute-start.12) | collective-permute-done | bytes 524320 | tf_op jit(solution)/shard_map/ppermute | solution.py:43
  136.9 3.5 %collective-permute-start.13 = (f32[2,64,4,1,128]{4,3,2,1,0:T(1,128)S(1)}, f32[2,64,4,1,128]{4,3,2,1,0:T(1,128)S(1)}, u32[]{:S(2)}, u32[]{:S(2)}) collective-permute-start(f32[2,64,4,1,128]{4,3,2,1,0:T(1,128)S(1)} %get-tuple-element.11), channel_id=1, source_target_pairs={{0,1},{1,2},{2,3},{4,5},{5,6},{6,7},{8,9},{9,10},{10,11},{12,13},{... | collective-permute-start | bytes 786440 | tf_op jit(solution)/shard_map/ppermute | solution.py:41
  141.7 2.6 %collective-permute-done.13 = f32[2,64,4,1,128]{4,3,2,1,0:T(1,128)S(1)} collective-permute-done((f32[2,64,4,1,128]{4,3,2,1,0:T(1,128)S(1)}, f32[2,64,4,1,128]{4,3,2,1,0:T(1,128)S(1)}, u32[]{:S(2)}, u32[]{:S(2)}) %collective-permute-start.13) | collective-permute-done | bytes 262176 | tf_op jit(solution)/shard_map/ppermute | solution.py:41
  144.3 4.4 %collective-permute-done.14 = f32[2,64,4,1,128]{4,3,2,1,0:T(1,128)S(1)} collective-permute-done((f32[2,64,4,1,128]{4,3,2,1,0:T(1,128)S(1)}, f32[2,64,4,1,128]{4,3,2,1,0:T(1,128)S(1)}, u32[]{:S(2)}, u32[]{:S(2)}) %collective-permute-start.14) | collective-permute-done | bytes 262176 | tf_op jit(solution)/shard_map/ppermute | solution.py:43
  148.7 6.7 %select_maximum_fusion.5 = f32[2,64,4,10,130]{4,3,2,1,0:T(8,128)S(1)} fusion(f32[2,64,4,1,128]{4,3,2,1,0:T(1,128)S(1)} %collective-permute-done.14, f32[2,64,4,1,128]{4,3,2,1,0:T(1,128)S(1)} %collective-permute-done.13, f32[2,64,1,8,128]{4,3,2,1,0:T(8,128)S(1)} %collective-permute-done.12, f32[2,64,1,8,128]{4,3,2,1,0:T(8,128)S(1)} %collective-permute-done.11, ...), kind=kLoop, calls=%fused_computation.8 | loop fusion | flops 9318400 | bytes 5283840 | tf_op jit(solution)/shard_map/concatenate | solution.py:39
  157.0 8.0 %collective-permute-start.15 = (f32[2,64,1,8,128]{4,3,2,1,0:T(8,128)S(1)}, f32[2,64,1,8,128]{4,3,2,1,0:T(8,128)S(1)}, u32[]{:S(2)}, u32[]{:S(2)}) collective-permute-start(f32[2,64,1,8,128]{4,3,2,1,0:T(8,128)S(1)} %get-tuple-element.31), channel_id=1, source_target_pairs={{0,4},{4,8},{8,12},{12,16},{16,20},{20,24},{24,28},{1,5},{5,9},{9,... | collective-permute-start | bytes 1572872 | tf_op jit(solution)/shard_map/ppermute | solution.py:41
  166.5 4.1 %collective-permute-done.16 = f32[2,64,1,8,128]{4,3,2,1,0:T(8,128)S(1)} collective-permute-done((f32[2,64,1,8,128]{4,3,2,1,0:T(8,128)S(1)}, f32[2,64,1,8,128]{4,3,2,1,0:T(8,128)S(1)}, u32[]{:S(2)}, u32[]{:S(2)}) %collective-permute-start.16) | collective-permute-done | bytes 524320 | tf_op jit(solution)/shard_map/ppermute | solution.py:43
  170.9 2.5 %collective-permute-start.17 = (f32[2,64,4,1,128]{4,3,2,1,0:T(1,128)S(1)}, f32[2,64,4,1,128]{4,3,2,1,0:T(1,128)S(1)}, u32[]{:S(2)}, u32[]{:S(2)}) collective-permute-start(f32[2,64,4,1,128]{4,3,2,1,0:T(1,128)S(1)} %get-tuple-element.9), channel_id=1, source_target_pairs={{0,1},{1,2},{2,3},{4,5},{5,6},{6,7},{8,9},{9,10},{10,11},{12,13},{... | collective-permute-start | bytes 786440 | tf_op jit(solution)/shard_map/ppermute | solution.py:41
  174.8 2.4 %collective-permute-done.17 = f32[2,64,4,1,128]{4,3,2,1,0:T(1,128)S(1)} collective-permute-done((f32[2,64,4,1,128]{4,3,2,1,0:T(1,128)S(1)}, f32[2,64,4,1,128]{4,3,2,1,0:T(1,128)S(1)}, u32[]{:S(2)}, u32[]{:S(2)}) %collective-permute-start.17) | collective-permute-done | bytes 262176 | tf_op jit(solution)/shard_map/ppermute | solution.py:41
  177.2 4.6 %collective-permute-done.18 = f32[2,64,4,1,128]{4,3,2,1,0:T(1,128)S(1)} collective-permute-done((f32[2,64,4,1,128]{4,3,2,1,0:T(1,128)S(1)}, f32[2,64,4,1,128]{4,3,2,1,0:T(1,128)S(1)}, u32[]{:S(2)}, u32[]{:S(2)}) %collective-permute-start.18) | collective-permute-done | bytes 262176 | tf_op jit(solution)/shard_map/ppermute | solution.py:43
  181.8 6.7 %select_maximum_fusion = f32[2,64,4,10,130]{4,3,2,1,0:T(8,128)S(1)} fusion(f32[2,64,4,1,128]{4,3,2,1,0:T(1,128)S(1)} %collective-permute-done.18, f32[2,64,4,1,128]{4,3,2,1,0:T(1,128)S(1)} %collective-permute-done.17, f32[2,64,1,8,128]{4,3,2,1,0:T(8,128)S(1)} %collective-permute-done.16, f32[2,64,1,8,128]{4,3,2,1,0:T(8,128)S(1)} %collective-permute-done.15, ...), kind=kLoop, calls=%fused_computation.3 | loop fusion | flops 9318400 | bytes 5283840 | tf_op jit(solution)/shard_map/concatenate | solution.py:39
  192.5 9.5 %all-to-all-start.1 = ((f32[64,2,8,128]{3,2,1,0:T(8,128)}), f32[64,2,8,128]{3,2,1,0:T(8,128)S(1)}, u32[]{:S(2)}, u32[]{:S(2)}) async-start(f32[64,2,8,128]{3,2,1,0:T(8,128)} %bitcast.48), calls=%async_computation.1 | async-start | bytes 1048576 | tf_op jit(solution)/shard_map/all_to_all | solution.py:139
  202.0 9.7 %all-to-all-done.1 = f32[64,2,8,128]{3,2,1,0:T(8,128)S(1)} async-done(((f32[64,2,8,128]{3,2,1,0:T(8,128)}), f32[64,2,8,128]{3,2,1,0:T(8,128)S(1)}, u32[]{:S(2)}, u32[]{:S(2)}) %all-to-all-start.1) | async-done | bytes 524320 | tf_op jit(solution)/shard_map/all_to_all | solution.py:139
  (107 shorter events, 42.5 us)
Async XLA Ops:
  1.2 10.0 %collective-permute-start = (f32[1,16,8,128]{3,1,2,0:T(8,128)S(1)}, f32[1,16,8,128]{3,1,2,0:T(8,128)S(1)}, u32[]{:S(2)}, u32[]{:S(2)}) collective-permute-start(f32[1,16,8,128]{3,1,2,0:T(8,128)S(1)} %slice.399), channel_id=1, source_target_pairs={{4,0},{8,4},{12,8},{16,12},{20,16},{24,20},{28,24},{5,1},{9,5},{13... | collective-permute-start | bytes 196616 | tf_op jit(solution)/shard_map/ppermute | solution.py:30
  9.6 23.3 %copy-start.3 = (f32[8,16,8,128]{3,2,1,0:T(8,128)S(1)}, f32[8,16,8,128]{3,2,1,0:T(8,128)}, u32[]{:S(2)}) copy-start(f32[8,16,8,128]{3,2,1,0:T(8,128)} %param.7) | copy-start | bytes 1572868
  11.1 18.5 %collective-permute-start.1 = (f32[14,16,1,128]{3,1,2,0:T(8,128)S(1)}, f32[14,16,1,128]{3,1,2,0:T(8,128)S(1)}, u32[]{:S(2)}, u32[]{:S(2)}) collective-permute-start(f32[14,16,1,128]{3,1,2,0:T(8,128)S(1)} %get-tuple-element.41), channel_id=1, source_target_pairs={{0,1},{1,2},{2,3},{4,5},{5,6},{6,7},{8,9},{9,10},{10,11},{12,13},{... | collective-permute-start | bytes 344072 | tf_op jit(solution)/shard_map/ppermute | solution.py:41
  16.1 13.5 %collective-permute-start.2 = (f32[14,16,1,128]{3,1,2,0:T(8,128)S(1)}, f32[14,16,1,128]{3,1,2,0:T(8,128)S(1)}, u32[]{:S(2)}, u32[]{:S(2)}) collective-permute-start(f32[14,16,1,128]{3,1,2,0:T(8,128)S(1)} %get-tuple-element.42), channel_id=1, source_target_pairs={{1,0},{2,1},{3,2},{5,4},{6,5},{7,6},{9,8},{10,9},{11,10},{13,12},{... | collective-permute-start | bytes 344072 | tf_op jit(solution)/shard_map/ppermute | solution.py:43
  31.1 1.7 copy-start
  33.9 33.1 %slice-start = ((f32[14,18,10,130]{3,1,2,0:T(8,128)}), f32[6,18,10,130]{3,1,2,0:T(8,128)S(1)}, s32[]{:S(2)}) async-start(f32[14,18,10,130]{3,1,2,0:T(8,128)} %copy-done), calls=%async_computation.2 | async-start | bytes 2949120 | tf_op jit(solution)/shard_map/slice | solution.py:111
  48.8 0.8 copy-start.5
  49.5 0.8 copy-start.7
  50.3 0.8 copy-start.1
  52.2 3.4 %collective-permute-start.3 = (f32[2,64,1,8,128]{4,3,2,1,0:T(8,128)}, f32[2,64,1,8,128]{4,3,2,1,0:T(8,128)}, u32[]{:S(2)}, u32[]{:S(2)}) collective-permute-start(f32[2,64,1,8,128]{4,3,2,1,0:T(8,128)} %get-tuple-element.37), channel_id=1, source_target_pairs={{0,4},{4,8},{8,12},{12,16},{16,20},{20,24},{24,28},{1,5},{5,9},{9,... | collective-permute-start | bytes 1572872 | tf_op jit(solution)/shard_map/ppermute | solution.py:41
  54.3 4.1 %collective-permute-start.4 = (f32[2,64,1,8,128]{4,3,2,1,0:T(8,128)}, f32[2,64,1,8,128]{4,3,2,1,0:T(8,128)}, u32[]{:S(2)}, u32[]{:S(2)}) collective-permute-start(f32[2,64,1,8,128]{4,3,2,1,0:T(8,128)} %get-tuple-element.38), channel_id=1, source_target_pairs={{4,0},{8,4},{12,8},{16,12},{20,16},{24,20},{28,24},{5,1},{9,5},{13... | collective-permute-start | bytes 1572872 | tf_op jit(solution)/shard_map/ppermute | solution.py:43
  61.0 8.7 %collective-permute-start.5 = (f32[2,64,4,1,128]{4,3,2,1,0:T(1,128)}, f32[2,64,4,1,128]{4,3,2,1,0:T(1,128)S(1)}, u32[]{:S(2)}, u32[]{:S(2)}) collective-permute-start(f32[2,64,4,1,128]{4,3,2,1,0:T(1,128)} %get-tuple-element.15), channel_id=1, source_target_pairs={{0,1},{1,2},{2,3},{4,5},{5,6},{6,7},{8,9},{9,10},{10,11},{12,13},{... | collective-permute-start | bytes 786440 | tf_op jit(solution)/shard_map/ppermute | solution.py:41
  65.6 8.6 %collective-permute-start.6 = (f32[2,64,4,1,128]{4,3,2,1,0:T(1,128)}, f32[2,64,4,1,128]{4,3,2,1,0:T(1,128)}, u32[]{:S(2)}, u32[]{:S(2)}) collective-permute-start(f32[2,64,4,1,128]{4,3,2,1,0:T(1,128)} %get-tuple-element.16), channel_id=1, source_target_pairs={{1,0},{2,1},{3,2},{5,4},{6,5},{7,6},{9,8},{10,9},{11,10},{13,12},{... | collective-permute-start | bytes 786440 | tf_op jit(solution)/shard_map/ppermute | solution.py:43
  67.2 16.6 %copy-start.2 = (f32[8,8,16,128]{3,2,1,0:T(8,128)S(1)}, f32[8,8,16,128]{3,2,1,0:T(8,128)}, u32[]{:S(2)}) copy-start(f32[8,8,16,128]{3,2,1,0:T(8,128)} %copy-done.1) | copy-start | bytes 1572868
  84.1 12.2 %collective-permute-start.7 = (f32[2,64,1,8,128]{4,3,2,1,0:T(8,128)S(1)}, f32[2,64,1,8,128]{4,3,2,1,0:T(8,128)S(1)}, u32[]{:S(2)}, u32[]{:S(2)}) collective-permute-start(f32[2,64,1,8,128]{4,3,2,1,0:T(8,128)S(1)} %get-tuple-element.35), channel_id=1, source_target_pairs={{0,4},{4,8},{8,12},{12,16},{16,20},{20,24},{24,28},{1,5},{5,9},{9,... | collective-permute-start | bytes 1572872 | tf_op jit(solution)/shard_map/ppermute | solution.py:41
  94.8 6.7 %collective-permute-start.8 = (f32[2,64,1,8,128]{4,3,2,1,0:T(8,128)S(1)}, f32[2,64,1,8,128]{4,3,2,1,0:T(8,128)S(1)}, u32[]{:S(2)}, u32[]{:S(2)}) collective-permute-start(f32[2,64,1,8,128]{4,3,2,1,0:T(8,128)S(1)} %get-tuple-element.36), channel_id=1, source_target_pairs={{4,0},{8,4},{12,8},{16,12},{20,16},{24,20},{28,24},{5,1},{9,5},{13... | collective-permute-start | bytes 1572872 | tf_op jit(solution)/shard_map/ppermute | solution.py:43
  101.9 7.4 %collective-permute-start.9 = (f32[2,64,4,1,128]{4,3,2,1,0:T(1,128)S(1)}, f32[2,64,4,1,128]{4,3,2,1,0:T(1,128)S(1)}, u32[]{:S(2)}, u32[]{:S(2)}) collective-permute-start(f32[2,64,4,1,128]{4,3,2,1,0:T(1,128)S(1)} %get-tuple-element.13), channel_id=1, source_target_pairs={{0,1},{1,2},{2,3},{4,5},{5,6},{6,7},{8,9},{9,10},{10,11},{12,13},{... | collective-permute-start | bytes 786440 | tf_op jit(solution)/shard_map/ppermute | solution.py:41
  105.4 8.3 %collective-permute-start.10 = (f32[2,64,4,1,128]{4,3,2,1,0:T(1,128)S(1)}, f32[2,64,4,1,128]{4,3,2,1,0:T(1,128)S(1)}, u32[]{:S(2)}, u32[]{:S(2)}) collective-permute-start(f32[2,64,4,1,128]{4,3,2,1,0:T(1,128)S(1)} %get-tuple-element.14), channel_id=1, source_target_pairs={{1,0},{2,1},{3,2},{5,4},{6,5},{7,6},{9,8},{10,9},{11,10},{13,12},{... | collective-permute-start | bytes 786440 | tf_op jit(solution)/shard_map/ppermute | solution.py:43
  122.0 10.5 %collective-permute-start.11 = (f32[2,64,1,8,128]{4,3,2,1,0:T(8,128)S(1)}, f32[2,64,1,8,128]{4,3,2,1,0:T(8,128)S(1)}, u32[]{:S(2)}, u32[]{:S(2)}) collective-permute-start(f32[2,64,1,8,128]{4,3,2,1,0:T(8,128)S(1)} %get-tuple-element.33), channel_id=1, source_target_pairs={{0,4},{4,8},{8,12},{12,16},{16,20},{20,24},{24,28},{1,5},{5,9},{9,... | collective-permute-start | bytes 1572872 | tf_op jit(solution)/shard_map/ppermute | solution.py:41
  131.0 5.6 %collective-permute-start.12 = (f32[2,64,1,8,128]{4,3,2,1,0:T(8,128)S(1)}, f32[2,64,1,8,128]{4,3,2,1,0:T(8,128)S(1)}, u32[]{:S(2)}, u32[]{:S(2)}) collective-permute-start(f32[2,64,1,8,128]{4,3,2,1,0:T(8,128)S(1)} %get-tuple-element.34), channel_id=1, source_target_pairs={{4,0},{8,4},{12,8},{16,12},{20,16},{24,20},{28,24},{5,1},{9,5},{13... | collective-permute-start | bytes 1572872 | tf_op jit(solution)/shard_map/ppermute | solution.py:43
  136.9 7.3 %collective-permute-start.13 = (f32[2,64,4,1,128]{4,3,2,1,0:T(1,128)S(1)}, f32[2,64,4,1,128]{4,3,2,1,0:T(1,128)S(1)}, u32[]{:S(2)}, u32[]{:S(2)}) collective-permute-start(f32[2,64,4,1,128]{4,3,2,1,0:T(1,128)S(1)} %get-tuple-element.11), channel_id=1, source_target_pairs={{0,1},{1,2},{2,3},{4,5},{5,6},{6,7},{8,9},{9,10},{10,11},{12,13},{... | collective-permute-start | bytes 786440 | tf_op jit(solution)/shard_map/ppermute | solution.py:41
  140.4 8.3 %collective-permute-start.14 = (f32[2,64,4,1,128]{4,3,2,1,0:T(1,128)S(1)}, f32[2,64,4,1,128]{4,3,2,1,0:T(1,128)S(1)}, u32[]{:S(2)}, u32[]{:S(2)}) collective-permute-start(f32[2,64,4,1,128]{4,3,2,1,0:T(1,128)S(1)} %get-tuple-element.12), channel_id=1, source_target_pairs={{1,0},{2,1},{3,2},{5,4},{6,5},{7,6},{9,8},{10,9},{11,10},{13,12},{... | collective-permute-start | bytes 786440 | tf_op jit(solution)/shard_map/ppermute | solution.py:43
  157.0 9.5 %collective-permute-start.15 = (f32[2,64,1,8,128]{4,3,2,1,0:T(8,128)S(1)}, f32[2,64,1,8,128]{4,3,2,1,0:T(8,128)S(1)}, u32[]{:S(2)}, u32[]{:S(2)}) collective-permute-start(f32[2,64,1,8,128]{4,3,2,1,0:T(8,128)S(1)} %get-tuple-element.31), channel_id=1, source_target_pairs={{0,4},{4,8},{8,12},{12,16},{16,20},{20,24},{24,28},{1,5},{5,9},{9,... | collective-permute-start | bytes 1572872 | tf_op jit(solution)/shard_map/ppermute | solution.py:41
  165.0 5.5 %collective-permute-start.16 = (f32[2,64,1,8,128]{4,3,2,1,0:T(8,128)S(1)}, f32[2,64,1,8,128]{4,3,2,1,0:T(8,128)S(1)}, u32[]{:S(2)}, u32[]{:S(2)}) collective-permute-start(f32[2,64,1,8,128]{4,3,2,1,0:T(8,128)S(1)} %get-tuple-element.32), channel_id=1, source_target_pairs={{4,0},{8,4},{12,8},{16,12},{20,16},{24,20},{28,24},{5,1},{9,5},{13... | collective-permute-start | bytes 1572872 | tf_op jit(solution)/shard_map/ppermute | solution.py:43
  170.9 6.3 %collective-permute-start.17 = (f32[2,64,4,1,128]{4,3,2,1,0:T(1,128)S(1)}, f32[2,64,4,1,128]{4,3,2,1,0:T(1,128)S(1)}, u32[]{:S(2)}, u32[]{:S(2)}) collective-permute-start(f32[2,64,4,1,128]{4,3,2,1,0:T(1,128)S(1)} %get-tuple-element.9), channel_id=1, source_target_pairs={{0,1},{1,2},{2,3},{4,5},{5,6},{6,7},{8,9},{9,10},{10,11},{12,13},{... | collective-permute-start | bytes 786440 | tf_op jit(solution)/shard_map/ppermute | solution.py:41
  173.4 16.6 %copy-start.8 = (f32[64,2048]{1,0:T(8,128)S(1)}, f32[64,2048]{1,0:T(8,128)}, u32[]{:S(2)}) copy-start(f32[64,2048]{1,0:T(8,128)} %copy-done.7) | copy-start | bytes 1572868
  173.4 8.4 %collective-permute-start.18 = (f32[2,64,4,1,128]{4,3,2,1,0:T(1,128)S(1)}, f32[2,64,4,1,128]{4,3,2,1,0:T(1,128)S(1)}, u32[]{:S(2)}, u32[]{:S(2)}) collective-permute-start(f32[2,64,4,1,128]{4,3,2,1,0:T(1,128)S(1)} %get-tuple-element.10), channel_id=1, source_target_pairs={{1,0},{2,1},{3,2},{5,4},{6,5},{7,6},{9,8},{10,9},{11,10},{13,12},{... | collective-permute-start | bytes 786440 | tf_op jit(solution)/shard_map/ppermute | solution.py:43
  188.5 2.3 %copy-start.6 = (f32[64,2048]{1,0:T(8,128)S(1)}, f32[64,2048]{1,0:T(8,128)}, u32[]{:S(2)}) copy-start(f32[64,2048]{1,0:T(8,128)} %copy-done.5) | copy-start | bytes 1572868
  188.5 23.2 %copy-start.4 = (f32[8,16,8,128]{3,2,1,0:T(8,128)S(1)}, f32[8,16,8,128]{3,2,1,0:T(8,128)}, u32[]{:S(2)}) copy-start(f32[8,16,8,128]{3,2,1,0:T(8,128)} %param.7) | copy-start | bytes 1572868
  192.5 19.2 %all-to-all-start.1 = ((f32[64,2,8,128]{3,2,1,0:T(8,128)}), f32[64,2,8,128]{3,2,1,0:T(8,128)S(1)}, u32[]{:S(2)}, u32[]{:S(2)}) async-start(f32[64,2,8,128]{3,2,1,0:T(8,128)} %bitcast.48), calls=%async_computation.1 | async-start | bytes 1048576 | tf_op jit(solution)/shard_map/all_to_all | solution.py:139
